TPU v7x, 512 devices: a whole 4x4x16 slice. The times are simulated.
512 devices in a mesh: tile: 16 (over y, x), cuts: 32 (over z, core).
Axes of the slice: x: 4, y: 4, z: 16, core: 2. Of those that a mesh axis runs over, the one named last changes fastest.
Arguments:
- density: bfloat16 [128, 2048, 1024], P('cuts', 'tile'), may hold values from -8 to 8
- valid: int32 [2048, 1024], P('tile'), may hold values from 0 to 1, as said below
- row_taps: bfloat16 [4, 128, 17], P(None, 'cuts'), may hold values from -1.5 to 1.5
- col_taps: bfloat16 [4, 128, 17], P(None, 'cuts'), may hold values from -1.5 to 1.5
- amp_matrix: bfloat16 [128, 128], replicated, may hold values from -0.5 to 0.5
- like_matrix: bfloat16 [128, 128], replicated, may hold values from -0.5 to 0.5
Outputs:
- amplitude: bfloat16 [128, 2097152], P(None, ('tile', 'cuts'))
- likelihood: bfloat16 [128, 2097152], P(None, ('tile', 'cuts'))
Inputs may be any that keep to these rules, and one draw needn't show every extreme that they name: Every pixel row holds at least one valid pixel; the share of valid pixels rises from about 0.3 in the first row to about 0.9 in the last.
All inputs are finite; a program needn't handle non-finite values.
Results may differ from a plain program's by a relative error of at most 0.0082.
Values may be sent and summed in bfloat16 or wider, within the bound.
A program may use at most 64 MiB of HBM per device.

v0:
```python
import jax
import jax.numpy as jnp
from jax import lax
from jax.sharding import PartitionSpec as P

REACH = 8
CBLK = 256


def extended(shard, sides, width):
    for axis, dim in sides:
        size, length = (lax.axis_size(axis), shard.shape[dim])
        up = [(i, (i + 1) % size) for i in range(size - 1)]
        down = [(j, i) for i, j in up]
        last = lax.slice_in_dim(shard, length - width, length, axis=dim)
        initial = lax.slice_in_dim(shard, 0, width, axis=dim)
        before = lax.ppermute(last, axis, up)
        after = lax.ppermute(initial, axis, down)
        shard = jnp.concatenate([before, shard, after], axis=dim)
    return shard


def band_matrix(taps, out_count, in_count):
    offset = lax.broadcasted_iota(jnp.int32, (out_count, in_count), 1) - lax.broadcasted_iota(
        jnp.int32, (out_count, in_count), 0
    )
    positions = lax.broadcasted_iota(jnp.int32, (1, 1, 2 * REACH + 1), 2)
    choose = (offset[:, :, None] == positions).astype(jnp.bfloat16)
    return jnp.einsum("ijt,kst->ksij", choose, taps, preferred_element_type=jnp.float32).astype(
        jnp.bfloat16
    )


def filter_field(padded, row_taps, col_taps):
    tall = padded.shape[1]
    col_count = padded.shape[2]
    row_band = band_matrix(row_taps, tall - 2 * REACH, tall)
    rowed = jnp.einsum(
        "ksij,sjc->ksic", row_band, padded, preferred_element_type=jnp.float32
    ).astype(jnp.bfloat16)
    widened = jnp.pad(rowed, ((0, 0), (0, 0), (0, 0), (REACH, REACH)))
    col_band = band_matrix(col_taps, CBLK, CBLK + 2 * REACH)
    pieces = []
    for begin in range(0, col_count, CBLK):
        segment = widened[:, :, :, begin : begin + CBLK + 2 * REACH]
        pieces.append(
            jnp.einsum("ksrj,ksij->sri", segment, col_band, preferred_element_type=jnp.float32)
        )
    return jnp.concatenate(pieces, axis=2).astype(jnp.bfloat16)


def project_pencil(pencil, amp_matrix, like_matrix):
    amp_float = jnp.dot(amp_matrix.T, pencil, preferred_element_type=jnp.float32)
    like_float = amp_float * jnp.dot(like_matrix.T, pencil, preferred_element_type=jnp.float32)
    return (amp_float.astype(jnp.bfloat16), like_float.astype(jnp.bfloat16))


def global_background(local_sums, local_count):
    totals, counted = lax.psum((local_sums, local_count), "tile")
    return totals / counted


def per_device(density, valid, row_taps, col_taps, amp_matrix, like_matrix):
    slice_count, row_count, col_count = density.shape
    mask_float = valid.astype(jnp.float32)
    local_sums = jnp.sum(density.astype(jnp.float32) * mask_float[None], axis=(1, 2))
    local_count = jnp.sum(mask_float)
    background = global_background(local_sums, local_count)
    masked_field = (
        mask_float[None] * (density.astype(jnp.float32) - background[:, None, None])
    ).astype(jnp.bfloat16)
    padded = extended(masked_field, (("tile", 1),), REACH)
    filtered = filter_field(padded, row_taps, col_taps)
    peers = lax.axis_size("cuts")
    share = row_count * col_count // peers
    split_flat = filtered.reshape(slice_count, peers, share)
    pencil = lax.all_to_all(split_flat, "cuts", split_axis=1, concat_axis=0, tiled=True).reshape(
        slice_count * peers, share
    )
    amplitude, likelihood = project_pencil(pencil, amp_matrix, like_matrix)
    return (amplitude, likelihood)


def solution(mesh):
    return jax.shard_map(
        per_device,
        mesh=mesh,
        in_specs=(
            P("cuts", "tile", None),
            P("tile", None),
            P(None, "cuts", None),
            P(None, "cuts", None),
            P(),
            P(),
        ),
        out_specs=(P(None, ("tile", "cuts")), P(None, ("tile", "cuts"))),
        check_vma=False,
    )
```

profile of v0, /device:TPU:1, one launch (start us, length us, event | category | flops | bytes accessed | tf_op | source)
XLA Modules:
  0.0 140.7 jit_solution(9057585749341689977)
XLA Ops:
  0.6 0.0 copy-start
  0.6 0.0 copy-start.2
  0.7 0.0 copy-start.1
  0.7 1.2 convert_element_type.49
  1.9 1.6 %fusion.6 = f32[4]{0:T(128)S(1)} fusion(bf16[4,128,1024]{2,1,0:T(8,128)(2,1)} %param.6, f32[128,1024]{1,0:T(8,128)S(1)} %convert_element_type.49), kind=kLoop, calls=%fused_computation.13 | loop fusion | flops 1572860 | bytes 1572880 | tf_op jit(solution)/shard_map/reduce_sum | solution.py:66
  3.5 0.0 copy-done.2
  3.5 0.7 convert_reduce_fusion
  4.2 34.9 %all-reduce.1 = (f32[4]{0:T(128)S(1)}, f32[]{:T(128)}) all-reduce(f32[4]{0:T(128)S(1)} %fusion.6, f32[]{:T(128)} %convert_reduce_fusion), channel_id=1, replica_groups=mesh['tile'=16,'cuts'=32] {'tile'}, use_global_device_ids=true, to_apply=%region_1.0 | all-reduce | flops 5 | bytes 40 | tf_op jit(solution)/shard_map/psum | solution.py:59
  39.1 0.6 broadcast_divide_fusion
  39.7 0.0 copy-done.1
  39.7 0.0 copy-start.4
  39.7 0.4 fusion.8
  40.1 1.3 collective-permute-start
  41.4 0.0 copy-start.5
  41.4 1.3 collective-permute-start.1
  42.8 0.2 fusion.20
  43.0 1.5 %copy.30 = pred[128,144,17,1]{1,2,3,0:T(8,128)(4,1)S(1)} copy(pred[128,144,17,1]{0,1,2,3:T(8,128)(4,1)S(1)} %fusion.20) | data formatting | bytes 626688 | tf_op jit(solution)/shard_map/eq | solution.py:28
  44.5 0.0 copy-done.4
  44.5 1.7 %convert_bitcast_fusion.1 = bf16[4,4,256,272]{2,1,0,3:T(4,128)(2,1)S(1)} fusion(s32[256,272]{0,1:T(8,128)S(1)} %iota_subtract_fusion, bf16[4,4,17]{2,1,0:T(4,128)(2,1)S(1)} %copy-done.4), kind=kOutput, calls=%fused_computation.12 | convolution fusion | flops 40177664 | bytes 2507296 | tf_op jit(solution)/shard_map/ijt,kst->ksij/dot_general | solution.py:29
  46.1 0.0 copy-done.5
  46.2 0.7 fusion.19
  46.9 0.0 collective-permute-done
  46.9 0.0 collective-permute-done.1
  46.9 2.0 %convert_bitcast_fusion = bf16[4,4,128,1024]{2,3,0,1:T(8,128)(2,1)S(1)} fusion(bf16[4,8,1024]{2,1,0:T(8,128)(2,1)S(1)} %collective-permute-done.1, bf16[4,128,1024]{2,1,0:T(8,128)(2,1)S(1)} %fusion.8, bf16[4,8,1024]{2,1,0:T(8,128)(2,1)S(1)} %collective-permute-done, bf16[4,4,128,144]{3,1,0,2:T(4,128)(2,1)S(1)} %fusion.19), kind=kOutput, calls=%fused_computation.6 | convolution fusion | flops 609615872 | bytes 5963776 | tf_op jit(solution)/shard_map/ksij,sjc->ksic/dot_general | solution.py:38
  48.9 1.6 %fusion.42 = bf16[4,128,256]{2,1,0:T(8,128)(2,1)S(1)} fusion(bf16[4,4,256,272]{2,1,0,3:T(4,128)(2,1)S(1)} %convert_bitcast_fusion.1, bf16[4,4,128,1024]{2,3,0,1:T(8,128)(2,1)S(1)} %convert_bitcast_fusion), kind=kOutput, calls=%fused_computation.35 | convolution fusion | flops 285343744 | bytes 6684672 | tf_op jit(solution)/shard_map/ksrj,ksij->sri/dot_general | solution.py:47
  50.4 1.6 %fusion.39 = bf16[4,128,256]{2,1,0:T(8,128)(2,1)S(1)} fusion(bf16[4,4,256,272]{2,1,0,3:T(4,128)(2,1)S(1)} %convert_bitcast_fusion.1, bf16[4,4,128,1024]{2,3,0,1:T(8,128)(2,1)S(1)} %convert_bitcast_fusion), kind=kOutput, calls=%fused_computation.34 | convolution fusion | flops 285343744 | bytes 3604480 | tf_op jit(solution)/shard_map/ksrj,ksij->sri/dot_general | solution.py:47
  52.0 1.6 %fusion.36 = bf16[4,128,256]{2,1,0:T(8,128)(2,1)S(1)} fusion(bf16[4,4,256,272]{2,1,0,3:T(4,128)(2,1)S(1)} %convert_bitcast_fusion.1, bf16[4,4,128,1024]{2,3,0,1:T(8,128)(2,1)S(1)} %convert_bitcast_fusion), kind=kOutput, calls=%fused_computation.33 | convolution fusion | flops 285343744 | bytes 3604480 | tf_op jit(solution)/shard_map/ksrj,ksij->sri/dot_general | solution.py:47
  53.6 1.6 %fusion.33 = bf16[4,128,256]{2,1,0:T(8,128)(2,1)S(1)} fusion(bf16[4,4,256,272]{2,1,0,3:T(4,128)(2,1)S(1)} %convert_bitcast_fusion.1, bf16[4,4,128,1024]{2,3,0,1:T(8,128)(2,1)S(1)} %convert_bitcast_fusion), kind=kOutput, calls=%fused_computation.32 | convolution fusion | flops 285343744 | bytes 6684672 | tf_op jit(solution)/shard_map/ksrj,ksij->sri/dot_general | solution.py:47
  55.1 0.1 pad_maximum_fusion
  55.3 0.7 convert_element_type.58
  55.9 0.8 copy.27
  56.8 79.3 %all_to_all.15 = bf16[4,32,4096]{2,0,1:T(4,128)(2,1)S(1)} all-to-all(bf16[4,32,4096]{2,0,1:T(4,128)(2,1)S(1)} %copy.27), channel_id=1, replica_groups=mesh['tile'=16,'cuts'=32] {'cuts'}, dimensions={1} | all-to-all | bytes 2097152 | tf_op jit(solution)/shard_map/all_to_all | solution.py:77
  136.1 0.3 reshape.27
  136.4 0.0 copy-done
  136.4 0.5 fusion.58
  136.9 0.0 copy-start.3
  136.9 0.1 convert_bitcast_fusion.2
  137.0 0.6 copy-done.3
  137.6 0.5 fusion.4
  138.1 1.3 copy.29
  139.4 1.3 copy.28
  (3 shorter events, 0.0 us)
Async XLA Ops:
  0.6 135.7 %copy-start = (bf16[128,128]{1,0:T(8,128)(2,1)S(1)}, bf16[128,128]{1,0:T(8,128)(2,1)}, u32[]{:S(2)}) copy-start(bf16[128,128]{1,0:T(8,128)(2,1)} %param.10) | copy-start | bytes 98308
  0.6 2.8 %copy-start.2 = (s32[128,1024]{1,0:T(8,128)S(1)}, s32[128,1024]{1,0:T(8,128)}, u32[]{:S(2)}) copy-start(s32[128,1024]{1,0:T(8,128)} %param.7) | copy-start | bytes 1572868
  0.7 39.1 %copy-start.1 = (bf16[4,128,1024]{2,1,0:T(8,128)(2,1)S(1)}, bf16[4,128,1024]{2,1,0:T(8,128)(2,1)}, u32[]{:S(2)}) copy-start(bf16[4,128,1024]{2,1,0:T(8,128)(2,1)} %param.6) | copy-start | bytes 3145732
  39.7 4.7 %copy-start.4 = (bf16[4,4,17]{2,1,0:T(4,128)(2,1)S(1)}, bf16[4,4,17]{2,1,0:T(4,128)(2,1)}, u32[]{:S(2)}) copy-start(bf16[4,4,17]{2,1,0:T(4,128)(2,1)} %param.9) | copy-start | bytes 1636
  40.1 6.7 %collective-permute-start = (bf16[4,8,1024]{2,1,0:T(8,128)(2,1)S(1)}, bf16[4,8,1024]{2,1,0:T(8,128)(2,1)S(1)}, u32[]{:S(2)}, u32[]{:S(2)}) collective-permute-start(bf16[4,8,1024]{2,1,0:T(8,128)(2,1)S(1)} %get-tuple-element.10), channel_id=1, source_target_pairs={{0,32},{32,64},{64,96},{96,128},{128,160},{160,192},{192,224},{224... | collective-permute-start | bytes 196616 | tf_op jit(solution)/shard_map/ppermute | solution.py:17
  41.4 4.7 %copy-start.5 = (bf16[4,4,17]{2,1,0:T(4,128)(2,1)S(1)}, bf16[4,4,17]{2,1,0:T(4,128)(2,1)}, u32[]{:S(2)}) copy-start(bf16[4,4,17]{2,1,0:T(4,128)(2,1)} %param.8) | copy-start | bytes 1636
  41.4 5.4 %collective-permute-start.1 = (bf16[4,8,1024]{2,1,0:T(8,128)(2,1)S(1)}, bf16[4,8,1024]{2,1,0:T(8,128)(2,1)S(1)}, u32[]{:S(2)}, u32[]{:S(2)}) collective-permute-start(bf16[4,8,1024]{2,1,0:T(8,128)(2,1)S(1)} %get-tuple-element.11), channel_id=1, source_target_pairs={{32,0},{64,32},{96,64},{128,96},{160,128},{192,160},{224,192},{256... | collective-permute-start | bytes 196616 | tf_op jit(solution)/shard_map/ppermute | solution.py:18
  136.9 0.8 copy-start.3
where the time goes:
time: 141 us
  blocking collectives  114 us (81%)
  matrix products  11.6 us (8%)
  local copies, waits for them, and re-layouts  6.54 us (5%)
  other arithmetic  4.96 us (4%)
  starting transfers between devices  2.59 us (2%)
    all_to_all x1, blocking collectives, per_device(): lax.all_to_all(split_flat, 'cuts', split_axis=1, concat_axis=0, tiled=True)  79.3 us
    psum x1, blocking collectives, global_background(): totals, counted = lax.psum((local_sums, local_count), 'tile')  34.9 us
    dot_general x4, matrix products, filter_field(): jnp.einsum('ksrj,ksij->sri', segment, col_band, preferred_element_type=jn...  6.25 us
    unnamed x14, local copies, waits for them, and re-layouts  3.29 us
  transfers between devices with their start and end apart: 2, of which 0 were waited for; matrix products, arithmetic and copies ran while one was open for 3% of the time, Pallas kernels for 0%

commit v1 on v0

v1 whole, which is shorter than its diff:
```python
import functools

import jax
import jax.numpy as jnp
from jax import lax
from jax.experimental import pallas as pl
from jax.experimental.pallas import tpu as pltpu
from jax.sharding import PartitionSpec as P

MESH = pl.DeviceIdType.MESH
REACH = 8
TAPS = 2 * REACH + 1
ABSENT = 1024.0
F32 = jnp.float32
BF16 = jnp.bfloat16


def distance(p):
    return (8 - (p + 1) // 2) * (2 * (p % 2) - 1)


def exchange_kernel(
    dens, valid, rtap, ctap, amp, like,
    recv, wout,
    base, rband, cband, field, wide, outs, send, stat, stats, bgs, hsend, hrecv, wmat,
    stat_ssem, stat_rsem, halo_ssem, halo_rsem, ssem, rsem, wsem, osem,
):
    n_s, n_row, n_col = dens.shape
    n_tile, n_cut = lax.axis_size("tile"), lax.axis_size("cuts")
    n_z = n_cut // 2
    tile, me = lax.axis_index("tile"), lax.axis_index("cuts")
    z, core = me // 2, me % 2
    n_a = n_col // 128

    barrier = pltpu.get_barrier_semaphore()
    for i in range(1, n_tile):
        pl.semaphore_signal(barrier, inc=1, device_id={"tile": (tile + i) % n_tile}, device_id_type=MESH)
    for i in range(1, n_cut):
        pl.semaphore_signal(barrier, inc=1, device_id={"cuts": (me + i) % n_cut}, device_id_type=MESH)

    def fold(x):
        x = x[0:8] + x[8:16]
        total = x[:, 0:128]
        for a in range(1, n_a):
            total = total + x[:, 128 * a : 128 * a + 128]
        return total

    def sum_rows(i, accs):
        rows = pl.ds(pl.multiple_of(i * 16, 16), 16)
        mask = valid[rows, :].astype(F32)
        out = [accs[s] + fold(dens[s, rows, :].astype(F32) * mask) for s in range(n_s)]
        return (*out, accs[n_s] + fold(mask))

    accs = lax.fori_loop(0, n_row // 16, sum_rows, tuple(jnp.zeros((8, 128), F32) for _ in range(n_s + 1)))
    stat[...] = jnp.zeros_like(stat)
    for s in range(n_s + 1):
        stat[s : s + 1, :] = jnp.sum(accs[s], axis=0, keepdims=True)

    top, low = valid[0:8, :] != 0, valid[n_row - 8 : n_row, :] != 0
    for s in range(n_s):
        hsend[0, s] = jnp.where(top, dens[s, 0:16, :].astype(F32)[0:8], ABSENT).astype(BF16)
        hsend[1, s] = jnp.where(low, dens[s, n_row - 16 : n_row, :].astype(F32)[8:16], ABSENT).astype(BF16)

    pl.semaphore_wait(barrier, n_tile - 1 + n_cut - 1)

    stat_copies = []
    for i in range(1, n_tile):
        stat_copies.append(
            pltpu.make_async_remote_copy(
                stat, stats.at[i], stat_ssem.at[i], stat_rsem.at[i],
                device_id={"tile": (tile + i) % n_tile}, device_id_type=MESH,
            )
        )
    halo_copies = []
    for side, step in ((0, n_tile - 1), (1, 1)):
        halo_copies.append(
            pltpu.make_async_remote_copy(
                hsend.at[side], hrecv.at[side], halo_ssem.at[side], halo_rsem.at[side],
                device_id={"tile": (tile + step) % n_tile}, device_id_type=MESH,
            )
        )
    for copy in stat_copies + halo_copies:
        copy.start()

    base[...] = jnp.zeros_like(base)
    for k in range(4):
        base[4 * k : 4 * k + 4, 0:TAPS] = rtap[k].astype(F32)
        base[16 + 4 * k : 20 + 4 * k, 0:TAPS] = ctap[k].astype(F32)
    base[...] = pltpu.roll(base[...], 256 - REACH, 1)

    def build(k, carry):
        for s in range(n_s):
            row = jnp.broadcast_to(base[pl.ds(4 * k + s, 1), :], (8, 256))
            row = pltpu.roll(row, 0, 1, stride=1, stride_axis=0)
            if s % 2:
                row = pltpu.roll(row, 4, 0)
            for p in range(0, n_z, 2):
                pair = [pltpu.roll(row, 8 * ((z + distance(p + i) + n_z) % n_z), 1) for i in range(2)]
                rows = pl.ds(pl.multiple_of(32 * k + 8 * (p % 4), 16), 16)
                rband[s, p // 4, rows, :] = jnp.concatenate(pair, axis=0).astype(BF16)
            col = jnp.broadcast_to(base[pl.ds(16 + 4 * k + s, 1), :], (8, 256))
            col = pltpu.roll(col, 0, 1, stride=1, stride_axis=0)
            lanes = pl.ds(pl.multiple_of(256 * k, 256), 256)
            for m in range(0, 16, 2):
                pair = [pltpu.roll(col, 8 * (m + i), 1) if m + i else col for i in range(2)]
                cband[s, 8 * m : 8 * m + 16, lanes] = jnp.concatenate(pair, axis=0).astype(BF16)
        return carry

    lax.fori_loop(0, 4, build, 0)
    for s in range(n_s):
        field[s, n_row : 2 * n_row, :] = jnp.zeros((n_row, n_col), BF16)

    for copy in stat_copies:
        copy.wait()
    total = stat[...]
    for i in range(1, n_tile):
        total = total + stats[i]
    total = jnp.broadcast_to(jnp.sum(total, axis=1, keepdims=True), (8, 128))
    bgs[...] = total / jnp.broadcast_to(total[n_s : n_s + 1, :], (8, 128))

    def level(s):
        return jnp.concatenate([bgs[pl.ds(s, 1), :]] * n_a, axis=1)

    def mask_rows(i, carry):
        rows = pl.ds(pl.multiple_of(i * 16, 16), 16)
        mask = valid[rows, :].astype(F32)
        for s in range(n_s):
            field[s, rows, :] = (mask * (dens[s, rows, :].astype(F32) - level(s))).astype(BF16)
        return carry

    lax.fori_loop(0, n_row // 16, mask_rows, 0)
    for copy in halo_copies:
        copy.wait()
    has_after = (tile < n_tile - 1).astype(F32)
    has_before = (tile > 0).astype(F32)
    for s in range(n_s):
        after, before = hrecv[0, s].astype(F32), hrecv[1, s].astype(F32)
        after = jnp.where(after > 0.5 * ABSENT, 0.0, after - level(s)) * has_after
        before = jnp.where(before > 0.5 * ABSENT, 0.0, before - level(s)) * has_before
        none = jnp.zeros((8, n_col), F32)
        field[s, n_row : n_row + 16, :] = jnp.concatenate([after, none], axis=0).astype(BF16)
        field[s, 2 * n_row - 16 : 2 * n_row, :] = jnp.concatenate([none, before], axis=0).astype(BF16)

    def block_copy(p, c):
        target = 2 * ((z + distance(p) + n_z) % n_z) + c
        return pltpu.make_async_remote_copy(
            send.at[p, c], recv.at[p, core], ssem.at[p, c], rsem.at[p, core],
            device_id={"cuts": target}, device_id_type=MESH,
        )

    lane = lax.broadcasted_iota(jnp.int32, (32, 128), 1)
    first = lax.broadcasted_iota(jnp.int32, (8, 128), 0) < 4

    def chunk(q, carry):
        for s in range(n_s):
            rowed = jnp.dot(rband[s, q], field[s], preferred_element_type=F32)
            for k in range(4):
                tiles = [rowed[32 * k : 32 * k + 32, 128 * a : 128 * a + 128] for a in range(n_a)]
                for a in range(n_a):
                    right = tiles[a + 1] if a + 1 < n_a else jnp.zeros((32, 128), F32)
                    left = tiles[a - 1] if a else jnp.zeros((32, 128), F32)
                    wide[s, a, :, 256 * k : 256 * k + 128] = tiles[a].astype(BF16)
                    wide[s, a, :, 256 * k + 128 : 256 * k + 256] = jnp.where(lane < 64, right, left).astype(BF16)
            done = lax.dot_general(
                wide[s].reshape(32 * n_a, 1024), cband[s], (((1,), (1,)), ((), ())), preferred_element_type=F32
            )
            outs[s] = done.reshape(n_a, 32, 128)
        for i in range(4):
            p = 4 * q + i
            for a in range(n_a):
                part = [outs[s, a, 8 * i : 8 * i + 8, :] for s in range(n_s)]
                even = [jnp.where(first, part[0], part[1]), jnp.where(first, part[2], part[3])]
                odd = [jnp.where(first, part[1], part[0]), jnp.where(first, part[3], part[2])]
                send[p, 0, :, 128 * a : 128 * a + 128] = jnp.concatenate(even, axis=0).astype(BF16)
                send[p, 1, :, 128 * a : 128 * a + 128] = jnp.concatenate(odd, axis=0).astype(BF16)
        for i in range(4):
            p = 4 * q + i
            for c in range(2):

                @pl.when(jnp.logical_or(p < n_z - 1, c != core))
                def _():
                    block_copy(p, c).start()

        return carry

    lax.fori_loop(0, n_z // 4, chunk, 0)
    own = pltpu.make_async_copy(send.at[n_z - 1, core], recv.at[n_z - 1, core], osem)
    own.start()

    both = jnp.concatenate([amp[...].astype(F32).T, like[...].astype(F32).T], axis=0).astype(BF16)
    at = lax.broadcasted_iota(jnp.int32, (8, 512), 1)
    pos = at >> 5
    dist = (8 - ((pos + 1) >> 1)) * (2 * (pos & 1) - 1)
    inner = (at >> 2) & 3
    inner = inner + core * (1 - 2 * (inner & 1))
    slices = 8 * ((z - dist + 2 * n_z) & (n_z - 1)) + 4 * ((at >> 4) & 1) + inner
    slices = jnp.concatenate([slices] * 16, axis=0)
    row_of = jnp.concatenate([at & 3] * 16, axis=0)
    wanted = slices == lax.broadcasted_iota(jnp.int32, (128, 512), 0)
    for r in range(4):
        pick = jnp.where(jnp.logical_and(wanted, row_of == r), 1.0, 0.0).astype(BF16)
        wmat[256 * r : 256 * r + 256, :] = jnp.dot(both, pick, preferred_element_type=F32).astype(BF16)
    put = pltpu.make_async_copy(wmat, wout, wsem)
    put.start()

    own.wait()
    put.wait()

    def finish(p, carry):
        for c in range(2):

            @pl.when(jnp.logical_or(p < n_z - 1, c != core))
            def _():
                block_copy(p, c).wait_send()
                pltpu.make_async_remote_copy(
                    send.at[p, c], recv.at[p, c], ssem.at[p, c], rsem.at[p, c],
                    device_id={"cuts": me}, device_id_type=MESH,
                ).wait_recv()

        return carry

    lax.fori_loop(0, n_z, finish, 0)


def project_kernel(blocks, weights, amp_out, like_out):
    for j in range(4):
        both = jnp.dot(weights[...], blocks[:, 256 * j : 256 * j + 256], preferred_element_type=F32)
        for r in range(4):
            amp_float = both[256 * r : 256 * r + 128]
            like_float = amp_float * both[256 * r + 128 : 256 * r + 256]
            at = 1024 * r + 256 * j
            amp_out[:, at : at + 256] = amp_float.astype(BF16)
            like_out[:, at : at + 256] = like_float.astype(BF16)


def per_device(density, valid, row_taps, col_taps, amp_matrix, like_matrix):
    vmem = pl.BlockSpec(memory_space=pltpu.VMEM)
    anywhere = pl.BlockSpec(memory_space=pl.ANY)
    dma = pltpu.SemaphoreType.DMA
    blocks, weights = pl.pallas_call(
        exchange_kernel,
        out_shape=(
            jax.ShapeDtypeStruct((16, 2, 16, 1024), BF16),
            jax.ShapeDtypeStruct((1024, 512), BF16),
        ),
        in_specs=[vmem] * 6,
        out_specs=(anywhere, anywhere),
        scratch_shapes=[
            pltpu.VMEM((32, 256), F32),
            pltpu.VMEM((4, 4, 128, 256), BF16),
            pltpu.VMEM((4, 128, 1024), BF16),
            pltpu.VMEM((4, 256, 1024), BF16),
            pltpu.VMEM((4, 8, 32, 1024), BF16),
            pltpu.VMEM((4, 8, 32, 128), F32),
            pltpu.VMEM((16, 2, 16, 1024), BF16),
            pltpu.VMEM((8, 128), F32),
            pltpu.VMEM((16, 8, 128), F32),
            pltpu.VMEM((8, 128), F32),
            pltpu.VMEM((2, 4, 8, 1024), BF16),
            pltpu.VMEM((2, 4, 8, 1024), BF16),
            pltpu.VMEM((1024, 512), BF16),
            dma((16,)), dma((16,)), dma((2,)), dma((2,)),
            dma((16, 2)), dma((16, 2)), dma, dma,
        ],
        compiler_params=pltpu.CompilerParams(collective_id=0, has_side_effects=True),
        name="filter_exchange",
    )(density, valid, row_taps, col_taps, amp_matrix, like_matrix)
    out = jax.ShapeDtypeStruct((128, 4096), BF16)
    return pl.pallas_call(
        project_kernel,
        out_shape=(out, out),
        in_specs=[vmem] * 2,
        out_specs=(vmem, vmem),
        name="project",
    )(blocks.reshape(512, 1024), weights)


def solution(mesh):
    return jax.shard_map(
        per_device,
        mesh=mesh,
        in_specs=(
            P("cuts", "tile", None),
            P("tile", None),
            P(None, "cuts", None),
            P(None, "cuts", None),
            P(),
            P(),
        ),
        out_specs=(P(None, ("tile", "cuts")), P(None, ("tile", "cuts"))),
        check_vma=False,
    )
```

time: 141 us -> 79 us (0.56)
  blocking collectives: 114 us -> 0 us
  Pallas kernels: 0 us -> 78.2 us
  matrix products: 11.6 us -> 0 us
  local copies, waits for them, and re-layouts: 6.54 us -> 0 us
  other arithmetic: 4.96 us -> 0 us
  starting transfers between devices: 2.59 us -> 0 us
    all_to_all x1 -> x0, blocking collectives: 79.3 us -> none  [per_device(): lax.all_to_all(split_flat, 'cuts', split_axis=1, concat_axis=0, tiled=True)]
    pallas_call x0 -> x2, Pallas kernels: none -> 78.2 us  [the longest x1 74.1 us: per_device(): pl.pallas_call(exchange_kernel, out_shape=(jax.ShapeDtypeStruct((16, 2, 1...]
    psum x1 -> x0, blocking collectives: 34.9 us -> none  [global_background(): totals, counted = lax.psum((local_sums, local_count), 'tile')]
    dot_general x9 -> x0, matrix products: 11.6 us -> none  [the longest x4 6.25 us: filter_field(): jnp.einsum('ksrj,ksij->sri', segment, col_band, preferred_element_type=jn...]
    unnamed x14 -> x0, local copies, waits for them, and re-layouts: 3.29 us -> none
    ppermute x2 -> x0, starting transfers between devices: 2.59 us -> none  [the longest x1 1.29 us: extended(): before = lax.ppermute(last, axis, up)]
    reduce_sum x2 -> x0, other arithmetic: 2.33 us -> none  [the longest x1 1.59 us: per_device(): jnp.sum(density.astype(jnp.float32) * mask_float[None], axis=(1, 2))]
    convert_element_type x3 -> x0, other arithmetic: 1.66 us -> none  [the longest x1 1.19 us: per_device(): mask_float = valid.astype(jnp.float32)]
  transfers between devices with their start and end apart: 2 -> 0, of which waited for: 0 -> 0; matrix products, arithmetic and copies ran while one was open for 3% -> 0% of each run, Pallas kernels for 0% -> 0%
where the time goes in v1:
time: 79 us; the launch traced here: 78.8 us
  Pallas kernels  78.2 us (99%)
    pallas_call x1, Pallas kernels, per_device(): pl.pallas_call(exchange_kernel, out_shape=(jax.ShapeDtypeStruct((16, 2, 1...  74.1 us
    pallas_call x1, Pallas kernels, per_device(): pl.pallas_call(project_kernel, out_shape=(out, out), in_specs=[vmem] * 2,...  4.08 us

profile of v1, /device:TPU:1, one launch (start us, length us, event | category | flops | bytes accessed | tf_op | source)
XLA Modules:
  0.0 78.8 jit_solution(10249941849407816897)
XLA Ops:
  0.6 74.1 %filter_exchange.1 = (bf16[16,2,16,1024]{3,2,1,0:T(8,128)(2,1)}, bf16[1024,512]{1,0:T(8,128)(2,1)}) custom-call(bf16[4,128,1024]{2,1,0:T(8,128)(2,1)} %dens.1, s32[128,1024]{1,0:T(8,128)} %valid.1, bf16[4,4,17]{2,1,0:T(4,128)(2,1)} %rtap.1, bf16[4,4,17]{2,1,0:T(4,128)(2,1)} %ctap.1, bf16[128,128]{1,0:T(8,128)(2,1)} %amp.1, bf16[128,128]{1,0:T(8,128)(2,1)} %like.1), custom_call_target="tpu_custom_call" | custom-call | tf_op jit(solution)/shard_map/filter_exchange/pallas_call | solution.py:240
  74.7 4.1 %project.1 = (bf16[128,4096]{1,0:T(8,128)(2,1)}, bf16[128,4096]{1,0:T(8,128)(2,1)}) custom-call(bf16[512,1024]{1,0:T(8,128)(2,1)} %bitcast.1, bf16[1024,512]{1,0:T(8,128)(2,1)} %get-tuple-element.5.weights), custom_call_target="tpu_custom_call" | custom-call | tf_op jit(solution)/shard_map/project/pallas_call | solution.py:269

commit v2 on v1

--- a/solution.py
+++ b/solution.py
@@ -20,10 +20,10 @@
 
 
 def exchange_kernel(
-    dens, valid, rtap, ctap, amp, like,
+    dens_in, valid_in, rtap, ctap, amp, like,
     recv, wout,
-    base, rband, cband, field, wide, outs, send, stat, stats, bgs, hsend, hrecv, wmat,
-    stat_ssem, stat_rsem, halo_ssem, halo_rsem, ssem, rsem, wsem, osem,
+    dens, valid, base, rband, cband, field, wide, outs, send, stat, stats, bgs, hsend, hrecv, wmat,
+    stat_ssem, stat_rsem, halo_ssem, halo_rsem, ssem, rsem, wsem, osem, vsem, dsem, up, down,
 ):
     n_s, n_row, n_col = dens.shape
     n_tile, n_cut = lax.axis_size("tile"), lax.axis_size("cuts")
@@ -32,11 +32,29 @@
     z, core = me // 2, me % 2
     n_a = n_col // 128
 
+    loads = [pltpu.make_async_copy(valid_in, valid, vsem)]
+    loads += [pltpu.make_async_copy(dens_in.at[s], dens.at[s], dsem.at[s]) for s in range(n_s)]
+    for load in loads:
+        load.start()
+
     barrier = pltpu.get_barrier_semaphore()
     for i in range(1, n_tile):
         pl.semaphore_signal(barrier, inc=1, device_id={"tile": (tile + i) % n_tile}, device_id_type=MESH)
-    for i in range(1, n_cut):
-        pl.semaphore_signal(barrier, inc=1, device_id={"cuts": (me + i) % n_cut}, device_id_type=MESH)
+    above, below = (z + 1) % n_z, (z + n_z - 1) % n_z
+    near = (2 * above, 2 * above + 1, 2 * below, 2 * below + 1, 2 * z + 1 - core)
+    for peer in near:
+        pl.semaphore_signal(barrier, inc=1, device_id={"cuts": peer}, device_id_type=MESH)
+
+    base[...] = jnp.zeros_like(base)
+    for k in range(4):
+        base[4 * k : 4 * k + 4, 0:TAPS] = rtap[k].astype(F32)
+        base[16 + 4 * k : 20 + 4 * k, 0:TAPS] = ctap[k].astype(F32)
+    base[...] = pltpu.roll(base[...], 256 - REACH, 1)
+    for s in range(n_s):
+        field[s, n_row : 2 * n_row, :] = jnp.zeros((n_row, n_col), BF16)
+
+    for load in loads:
+        load.wait()
 
     def fold(x):
         x = x[0:8] + x[8:16]
@@ -61,7 +79,7 @@
         hsend[0, s] = jnp.where(top, dens[s, 0:16, :].astype(F32)[0:8], ABSENT).astype(BF16)
         hsend[1, s] = jnp.where(low, dens[s, n_row - 16 : n_row, :].astype(F32)[8:16], ABSENT).astype(BF16)
 
-    pl.semaphore_wait(barrier, n_tile - 1 + n_cut - 1)
+    pl.semaphore_wait(barrier, n_tile - 1 + len(near))
 
     stat_copies = []
     for i in range(1, n_tile):
@@ -82,13 +100,17 @@
     for copy in stat_copies + halo_copies:
         copy.start()
 
-    base[...] = jnp.zeros_like(base)
-    for k in range(4):
-        base[4 * k : 4 * k + 4, 0:TAPS] = rtap[k].astype(F32)
-        base[16 + 4 * k : 20 + 4 * k, 0:TAPS] = ctap[k].astype(F32)
-    base[...] = pltpu.roll(base[...], 256 - REACH, 1)
-
-    def build(k, carry):
+    def tell(d):
+        pl.semaphore_signal(up.at[d - 2], inc=1, device_id={"cuts": 2 * above + core}, device_id_type=MESH)
+        if d < n_z // 2:
+            pl.semaphore_signal(down.at[d - 2], inc=1, device_id={"cuts": 2 * below + core}, device_id_type=MESH)
+
+    def hear(d):
+        pl.semaphore_wait(up.at[d - 2], 1)
+        if d < n_z // 2:
+            pl.semaphore_wait(down.at[d - 2], 1)
+
+    def build(k):
         for s in range(n_s):
             row = jnp.broadcast_to(base[pl.ds(4 * k + s, 1), :], (8, 256))
             row = pltpu.roll(row, 0, 1, stride=1, stride_axis=0)
@@ -104,11 +126,12 @@
             for m in range(0, 16, 2):
                 pair = [pltpu.roll(col, 8 * (m + i), 1) if m + i else col for i in range(2)]
                 cband[s, 8 * m : 8 * m + 16, lanes] = jnp.concatenate(pair, axis=0).astype(BF16)
-        return carry
-
-    lax.fori_loop(0, 4, build, 0)
-    for s in range(n_s):
-        field[s, n_row : 2 * n_row, :] = jnp.zeros((n_row, n_col), BF16)
+
+    for d in range(2, 6):
+        tell(d)
+        build(d - 2)
+        hear(d)
+    tell(6)
 
     for copy in stat_copies:
         copy.wait()
@@ -129,6 +152,8 @@
         return carry
 
     lax.fori_loop(0, n_row // 16, mask_rows, 0)
+    hear(6)
+    tell(7)
     for copy in halo_copies:
         copy.wait()
     has_after = (tile < n_tile - 1).astype(F32)
@@ -151,20 +176,21 @@
     lane = lax.broadcasted_iota(jnp.int32, (32, 128), 1)
     first = lax.broadcasted_iota(jnp.int32, (8, 128), 0) < 4
 
-    def chunk(q, carry):
-        for s in range(n_s):
-            rowed = jnp.dot(rband[s, q], field[s], preferred_element_type=F32)
-            for k in range(4):
-                tiles = [rowed[32 * k : 32 * k + 32, 128 * a : 128 * a + 128] for a in range(n_a)]
-                for a in range(n_a):
-                    right = tiles[a + 1] if a + 1 < n_a else jnp.zeros((32, 128), F32)
-                    left = tiles[a - 1] if a else jnp.zeros((32, 128), F32)
-                    wide[s, a, :, 256 * k : 256 * k + 128] = tiles[a].astype(BF16)
-                    wide[s, a, :, 256 * k + 128 : 256 * k + 256] = jnp.where(lane < 64, right, left).astype(BF16)
-            done = lax.dot_general(
-                wide[s].reshape(32 * n_a, 1024), cband[s], (((1,), (1,)), ((), ())), preferred_element_type=F32
-            )
-            outs[s] = done.reshape(n_a, 32, 128)
+    def filtered(q, s):
+        rowed = jnp.dot(rband[s, q], field[s], preferred_element_type=F32)
+        for k in range(4):
+            tiles = [rowed[32 * k : 32 * k + 32, 128 * a : 128 * a + 128] for a in range(n_a)]
+            for a in range(n_a):
+                right = tiles[a + 1] if a + 1 < n_a else jnp.zeros((32, 128), F32)
+                left = tiles[a - 1] if a else jnp.zeros((32, 128), F32)
+                wide[s, a, :, 256 * k : 256 * k + 128] = tiles[a].astype(BF16)
+                wide[s, a, :, 256 * k + 128 : 256 * k + 256] = jnp.where(lane < 64, right, left).astype(BF16)
+        done = lax.dot_general(
+            wide[s].reshape(32 * n_a, 1024), cband[s], (((1,), (1,)), ((), ())), preferred_element_type=F32
+        )
+        outs[s] = done.reshape(n_a, 32, 128)
+
+    def pack(q):
         for i in range(4):
             p = 4 * q + i
             for a in range(n_a):
@@ -173,18 +199,28 @@
                 odd = [jnp.where(first, part[1], part[0]), jnp.where(first, part[3], part[2])]
                 send[p, 0, :, 128 * a : 128 * a + 128] = jnp.concatenate(even, axis=0).astype(BF16)
                 send[p, 1, :, 128 * a : 128 * a + 128] = jnp.concatenate(odd, axis=0).astype(BF16)
+
+    for s in range(n_s):
+        filtered(0, s)
+    pack(0)
+    hear(7)
+    tell(8)
+    hear(8)
+    for p in range(4):
+        for c in range(2):
+            block_copy(p, c).start()
+
+    def chunk(q, carry):
+        for s in range(n_s):
+            filtered(q, s)
+        pack(q)
         for i in range(4):
-            p = 4 * q + i
             for c in range(2):
-
-                @pl.when(jnp.logical_or(p < n_z - 1, c != core))
-                def _():
-                    block_copy(p, c).start()
-
+                pl.when(jnp.logical_or(4 * q + i < 15, c != core))(block_copy(4 * q + i, c).start)
         return carry
 
-    lax.fori_loop(0, n_z // 4, chunk, 0)
-    own = pltpu.make_async_copy(send.at[n_z - 1, core], recv.at[n_z - 1, core], osem)
+    lax.fori_loop(1, n_z // 4, chunk, 0)
+    own = pltpu.make_async_copy(send.at[15, core], recv.at[15, core], osem)
     own.start()
 
     both = jnp.concatenate([amp[...].astype(F32).T, like[...].astype(F32).T], axis=0).astype(BF16)
@@ -209,7 +245,7 @@
     def finish(p, carry):
         for c in range(2):
 
-            @pl.when(jnp.logical_or(p < n_z - 1, c != core))
+            @pl.when(jnp.logical_or(p < 15, c != core))
             def _():
                 block_copy(p, c).wait_send()
                 pltpu.make_async_remote_copy(
@@ -222,15 +258,23 @@
     lax.fori_loop(0, n_z, finish, 0)
 
 
-def project_kernel(blocks, weights, amp_out, like_out):
+def project_kernel(blocks, weights, amp_out, like_out, amps, likes, sems):
+    copies = []
     for j in range(4):
-        both = jnp.dot(weights[...], blocks[:, 256 * j : 256 * j + 256], preferred_element_type=F32)
+        part = blocks[:, :, :, 256 * j : 256 * j + 256].reshape(512, 256)
+        both = jnp.dot(weights[...], part, preferred_element_type=F32)
         for r in range(4):
             amp_float = both[256 * r : 256 * r + 128]
             like_float = amp_float * both[256 * r + 128 : 256 * r + 256]
-            at = 1024 * r + 256 * j
-            amp_out[:, at : at + 256] = amp_float.astype(BF16)
-            like_out[:, at : at + 256] = like_float.astype(BF16)
+            at = pl.ds(1024 * r + 256 * j, 256)
+            amps[:, at] = amp_float.astype(BF16)
+            likes[:, at] = like_float.astype(BF16)
+            for i, (kept, out) in enumerate(((amps, amp_out), (likes, like_out))):
+                copy = pltpu.make_async_copy(kept.at[:, at], out.at[:, at], sems.at[i, j, r])
+                copy.start()
+                copies.append(copy)
+    for copy in copies:
+        copy.wait()
 
 
 def per_device(density, valid, row_taps, col_taps, amp_matrix, like_matrix):
@@ -240,12 +284,14 @@
     blocks, weights = pl.pallas_call(
         exchange_kernel,
         out_shape=(
-            jax.ShapeDtypeStruct((16, 2, 16, 1024), BF16),
-            jax.ShapeDtypeStruct((1024, 512), BF16),
+            pltpu.VMEM((16, 2, 16, 1024), BF16),
+            pltpu.VMEM((1024, 512), BF16),
         ),
-        in_specs=[vmem] * 6,
-        out_specs=(anywhere, anywhere),
+        in_specs=[anywhere] * 2 + [vmem] * 4,
+        out_specs=(vmem, vmem),
         scratch_shapes=[
+            pltpu.VMEM((4, 128, 1024), BF16),
+            pltpu.VMEM((128, 1024), jnp.int32),
             pltpu.VMEM((32, 256), F32),
             pltpu.VMEM((4, 4, 128, 256), BF16),
             pltpu.VMEM((4, 128, 1024), BF16),
@@ -260,7 +306,8 @@
             pltpu.VMEM((2, 4, 8, 1024), BF16),
             pltpu.VMEM((1024, 512), BF16),
             dma((16,)), dma((16,)), dma((2,)), dma((2,)),
-            dma((16, 2)), dma((16, 2)), dma, dma,
+            dma((16, 2)), dma((16, 2)), dma, dma, dma, dma((4,)),
+            pltpu.SemaphoreType.REGULAR((8,)), pltpu.SemaphoreType.REGULAR((8,)),
         ],
         compiler_params=pltpu.CompilerParams(collective_id=0, has_side_effects=True),
         name="filter_exchange",
@@ -270,9 +317,13 @@
         project_kernel,
         out_shape=(out, out),
         in_specs=[vmem] * 2,
-        out_specs=(vmem, vmem),
+        out_specs=(anywhere, anywhere),
+        scratch_shapes=[pltpu.VMEM((128, 4096), BF16), pltpu.VMEM((128, 4096), BF16), dma((2, 4, 4))],
         name="project",
-    )(blocks.reshape(512, 1024), weights)
+    )(
+        pltpu.with_memory_space_constraint(blocks, pltpu.VMEM),
+        pltpu.with_memory_space_constraint(weights, pltpu.VMEM),
+    )
 
 
 def solution(mesh):

time: 79 us -> 76 us (0.962)
  Pallas kernels: 78.2 us -> 75.2 us
    pallas_call x1, Pallas kernels: 4.08 us -> 2.42 us  [per_device(): pl.pallas_call(project_kernel, out_shape=(out, out), in_specs=[vmem] * 2,...]
    pallas_call x1, Pallas kernels: 74.1 us -> 72.7 us  [per_device(): pl.pallas_call(exchange_kernel, out_shape=(pltpu.VMEM((16, 2, 16, 1024),...]
where the time goes in v2:
time: 76 us; the launch traced here: 75.8 us
  Pallas kernels  75.2 us (99%)
    pallas_call x1, Pallas kernels, per_device(): pl.pallas_call(exchange_kernel, out_shape=(pltpu.VMEM((16, 2, 16, 1024),...  72.7 us
    pallas_call x1, Pallas kernels, per_device(): pl.pallas_call(project_kernel, out_shape=(out, out), in_specs=[vmem] * 2,...  2.42 us

profile of v2, /device:TPU:1, one launch (start us, length us, event | category | flops | bytes accessed | tf_op | source)
XLA Modules:
  0.0 75.8 jit_solution(875788004586851839)
XLA Ops:
  0.6 72.7 %filter_exchange.1 = (bf16[16,2,16,1024]{3,2,1,0:T(8,128)(2,1)S(1)}, bf16[1024,512]{1,0:T(8,128)(2,1)S(1)}) custom-call(bf16[4,128,1024]{2,1,0:T(8,128)(2,1)} %dens_in.1, s32[128,1024]{1,0:T(8,128)} %valid_in.1, bf16[4,4,17]{2,1,0:T(4,128)(2,1)} %rtap.1, bf16[4,4,17]{2,1,0:T(4,128)(2,1)} %ctap.1, bf16[128,128]{1,0:T(8,128)(2,1)} %amp.1, bf16[128,128]{1,0:T(8,128)(2,1)} %like.1), custom_call_target="tpu_custom_call" | custom-call | tf_op jit(solution)/shard_map/filter_exchange/pallas_call | solution.py:284
  73.4 2.4 %project.1 = (bf16[128,4096]{1,0:T(8,128)(2,1)}, bf16[128,4096]{1,0:T(8,128)(2,1)}) custom-call(bf16[16,2,16,1024]{3,2,1,0:T(8,128)(2,1)S(1)} %get-tuple-element.4.blocks, bf16[1024,512]{1,0:T(8,128)(2,1)S(1)} %get-tuple-element.5.weights), custom_call_target="tpu_custom_call" | custom-call | tf_op jit(solution)/shard_map/project/pallas_call | solution.py:316

commit v3 on v2

v3 whole, which is shorter than its diff:
```python
import functools

import jax
import jax.numpy as jnp
from jax import lax
from jax.experimental import pallas as pl
from jax.experimental.pallas import tpu as pltpu
from jax.sharding import PartitionSpec as P

MESH = pl.DeviceIdType.MESH
REACH = 8
TAPS = 2 * REACH + 1
ABSENT = 1024.0
F32 = jnp.float32
BF16 = jnp.bfloat16

ORDER = (7, -7, 6, -6, 8, 5, -5, 4, -4, 3, -3, 2, -2, 1, -1, 0)
EARLY = 4
SELF = 15


def distance(p):
    return ORDER[p]


def exchange_kernel(
    dens_in, valid_in, rtap_in, ctap_in, amp_in, like_in,
    recv, wmat, acc,
    dens, valid, rtap, ctap, amp, like, base, rband, cband, field, wide, outs, send, stat, stats, bgs, hsend, hrecv,
    raw, local, delta, msg, msgs, seen, shifted, gmat,
    stat_ssem, stat_rsem, halo_ssem, halo_rsem, ssem, rsem, osem, vsem, dsem, small_sem, row_in, col_in, msg_ssem, msg_rsem,
):
    n_s, n_row, n_col = dens.shape
    n_tile, n_cut = lax.axis_size("tile"), lax.axis_size("cuts")
    n_z = n_cut // 2
    tile, me = lax.axis_index("tile"), lax.axis_index("cuts")
    z, core = me // 2, me % 2
    n_a = n_col // 128

    loads = [pltpu.make_async_copy(valid_in, valid, vsem)]
    loads += [pltpu.make_async_copy(dens_in.at[s], dens.at[s], dsem.at[s]) for s in range(n_s)]
    small = [(rtap_in, rtap), (ctap_in, ctap), (amp_in, amp), (like_in, like)]
    small = [pltpu.make_async_copy(a, b, small_sem.at[i]) for i, (a, b) in enumerate(small)]
    for load in small[:2] + loads + small[2:]:
        load.start()

    barrier = pltpu.get_barrier_semaphore()
    n_x = 4
    n_y = n_tile // n_x
    y, x = tile // n_x, tile % n_x
    left, right = n_x * y + (x + n_x - 1) % n_x, n_x * y + (x + 1) % n_x
    back, front = n_x * ((y + n_y - 1) % n_y) + x, n_x * ((y + 1) % n_y) + x
    def signal_tile(sem, peer):
        pl.semaphore_signal(sem, inc=1, device_id={"tile": peer}, device_id_type=MESH)

    for i in range(n_z // 2, -1, -1):
        for peer_z in (z + i, z + n_z - i)[: 1 if i % (n_z // 2) == 0 else 2]:
            for c in range(2 if i else 1):
                peer = 2 * (peer_z % n_z) + (c if i else 1 - core)
                pl.semaphore_signal(barrier, inc=1, device_id={"cuts": peer}, device_id_type=MESH)
    for peer in (left, right, back, front):
        signal_tile(barrier, peer)
    not_first, not_last = tile > 0, tile < n_tile - 1

    @pl.when(not_first)
    def _():
        signal_tile(barrier, tile - 1)

    @pl.when(not_last)
    def _():
        signal_tile(barrier, tile + 1)

    for load in small[:2]:
        load.wait()
    raw[...] = jnp.zeros_like(raw)
    for k in range(4):
        raw[4 * k : 4 * k + 4, 0:TAPS] = rtap[k].astype(F32)
        raw[16 + 4 * k : 20 + 4 * k, 0:TAPS] = ctap[k].astype(F32)
    base[...] = pltpu.roll(jnp.concatenate([raw[...], jnp.zeros_like(raw)], axis=1), 256 - REACH, 1)
    for s in range(n_s):
        field[s, n_row : 2 * n_row, :] = jnp.zeros((n_row, n_col), BF16)

    for load in loads:
        load.wait()

    def fold(x):
        x = x[0:8] + x[8:16]
        total = x[:, 0:128]
        for a in range(1, n_a):
            total = total + x[:, 128 * a : 128 * a + 128]
        return total

    def sum_rows(i, accs):
        rows = pl.ds(pl.multiple_of(i * 16, 16), 16)
        mask = valid[rows, :].astype(F32)
        out = [accs[s] + fold(dens[s, rows, :].astype(F32) * mask) for s in range(n_s)]
        return (*out, accs[n_s] + fold(mask))

    accs = lax.fori_loop(0, n_row // 16, sum_rows, tuple(jnp.zeros((8, 128), F32) for _ in range(n_s + 1)))
    stat[...] = jnp.zeros_like(stat)
    for s in range(n_s + 1):
        stat[s : s + 1, :] = jnp.sum(accs[s], axis=0, keepdims=True)

    def mean(total):
        total = jnp.broadcast_to(jnp.sum(total, axis=1, keepdims=True), (8, 128))
        return total / jnp.broadcast_to(total[n_s : n_s + 1, :], (8, 128))

    local[...] = mean(stat[...])

    top, low = valid[0:8, :] != 0, valid[n_row - 8 : n_row, :] != 0
    for s in range(n_s):
        hsend[0, s] = jnp.where(top, dens[s, 0:16, :].astype(F32)[0:8], ABSENT).astype(BF16)
        hsend[1, s] = jnp.where(low, dens[s, n_row - 16 : n_row, :].astype(F32)[8:16], ABSENT).astype(BF16)

    def build(k):
        for s in range(n_s):
            row = jnp.broadcast_to(base[pl.ds(4 * k + s, 1), :], (8, 256))
            row = pltpu.roll(row, 0, 1, stride=1, stride_axis=0)
            if s % 2:
                row = pltpu.roll(row, 4, 0)
            for p in range(0, n_z, 2):
                pair = [pltpu.roll(row, 8 * ((z + distance(p + i) + n_z) % n_z), 1) for i in range(2)]
                rows = pl.ds(pl.multiple_of(32 * k + 8 * (p % 4), 16), 16)
                rband[s, p // 4, rows, :] = jnp.concatenate(pair, axis=0).astype(BF16)
            col = jnp.broadcast_to(base[pl.ds(16 + 4 * k + s, 1), :], (8, 256))
            col = pltpu.roll(col, 0, 1, stride=1, stride_axis=0)
            lanes = pl.ds(pl.multiple_of(256 * k, 256), 256)
            for m in range(0, 16, 2):
                pair = [pltpu.roll(col, 8 * (m + i), 1) if m + i else col for i in range(2)]
                cband[s, 8 * m : 8 * m + 16, lanes] = jnp.concatenate(pair, axis=0).astype(BF16)

    for k in range(4):
        build(k)

    @pl.when(jnp.logical_not(not_last))
    def _():
        hrecv[0] = jnp.full((n_s, 8, n_col), ABSENT, BF16)

    @pl.when(jnp.logical_not(not_first))
    def _():
        hrecv[1] = jnp.full((n_s, 8, n_col), ABSENT, BF16)

    def fill_field(levels):
        def level(s):
            return jnp.concatenate([levels[pl.ds(s, 1), :]] * n_a, axis=1)

        def mask_rows(i, carry):
            rows = pl.ds(pl.multiple_of(i * 16, 16), 16)
            mask = valid[rows, :].astype(F32)
            for s in range(n_s):
                field[s, rows, :] = (mask * (dens[s, rows, :].astype(F32) - level(s))).astype(BF16)
            return carry

        lax.fori_loop(0, n_row // 16, mask_rows, 0)
        return level

    def fill_halo(level):
        for s in range(n_s):
            after, before = hrecv[0, s].astype(F32), hrecv[1, s].astype(F32)
            after = jnp.where(after > 0.5 * ABSENT, 0.0, after - level(s))
            before = jnp.where(before > 0.5 * ABSENT, 0.0, before - level(s))
            none = jnp.zeros((8, n_col), F32)
            field[s, n_row : n_row + 16, :] = jnp.concatenate([after, none], axis=0).astype(BF16)
            field[s, 2 * n_row - 16 : 2 * n_row, :] = jnp.concatenate([none, before], axis=0).astype(BF16)

    level = fill_field(local)

    def block_copy(p, c):
        target = 2 * ((z + distance(p) + n_z) % n_z) + c
        return pltpu.make_async_remote_copy(
            send.at[p, c], recv.at[p, core], ssem.at[p, c], rsem.at[p, core],
            device_id={"cuts": target}, device_id_type=MESH,
        )

    lane = lax.broadcasted_iota(jnp.int32, (32, 128), 1)
    first = lax.broadcasted_iota(jnp.int32, (8, 128), 0) < 4

    def filtered(q, s):
        rowed = jnp.dot(rband[s, q], field[s], preferred_element_type=F32)
        for k in range(4):
            tiles = [rowed[32 * k : 32 * k + 32, 128 * a : 128 * a + 128] for a in range(n_a)]
            for a in range(n_a):
                right = tiles[a + 1] if a + 1 < n_a else jnp.zeros((32, 128), F32)
                left = tiles[a - 1] if a else jnp.zeros((32, 128), F32)
                wide[s, a, :, 256 * k : 256 * k + 128] = tiles[a].astype(BF16)
                wide[s, a, :, 256 * k + 128 : 256 * k + 256] = jnp.where(lane < 64, right, left).astype(BF16)
        done = lax.dot_general(
            wide[s].reshape(32 * n_a, 1024), cband[s], (((1,), (1,)), ((), ())), preferred_element_type=F32
        )
        outs[s] = done.reshape(n_a, 32, 128)

    def pack_one(p):
        i = p % 4
        for a in range(n_a):
            part = [outs[s, a, 8 * i : 8 * i + 8, :] for s in range(n_s)]
            even = [jnp.where(first, part[0], part[1]), jnp.where(first, part[2], part[3])]
            odd = [jnp.where(first, part[1], part[0]), jnp.where(first, part[3], part[2])]
            send[p, 0, :, 128 * a : 128 * a + 128] = jnp.concatenate(even, axis=0).astype(BF16)
            send[p, 1, :, 128 * a : 128 * a + 128] = jnp.concatenate(odd, axis=0).astype(BF16)

    def start_one(p):
        for c in range(2):
            if p == SELF:
                pl.when(c != core)(block_copy(p, c).start)
            else:
                block_copy(p, c).start()

    def at_edge(p):
        target = (z + distance(p) + n_z) % n_z
        return jnp.logical_or(target == 0, target == n_z - 1)

    for s in range(n_s):
        filtered(0, s)
    for p in range(EARLY):
        pl.when(jnp.logical_not(at_edge(p)))(functools.partial(pack_one, p))

    pl.semaphore_wait(barrier, 4 + n_cut - 1 + not_first.astype(jnp.int32) + not_last.astype(jnp.int32))

    def halo_copy(side, peer):
        return pltpu.make_async_remote_copy(
            hsend.at[side], hrecv.at[side], halo_ssem.at[side], halo_rsem.at[side],
            device_id={"tile": peer}, device_id_type=MESH,
        )

    pl.when(not_first)(lambda: halo_copy(0, tile - 1).start())
    pl.when(not_last)(lambda: halo_copy(1, tile + 1).start())

    for p in range(EARLY):
        pl.when(jnp.logical_not(at_edge(p)))(functools.partial(start_one, p))

    @pl.when(not_first)
    def _():
        halo_copy(0, tile - 1).wait_send()
        halo_copy(1, tile - 1).wait_recv()

    @pl.when(not_last)
    def _():
        halo_copy(1, tile + 1).wait_send()
        halo_copy(0, tile + 1).wait_recv()

    fill_halo(level)
    for s in range(n_s):
        filtered(0, s)
    for p in range(EARLY):

        @pl.when(at_edge(p))
        def _():
            pack_one(p)
            start_one(p)

    stat_copies = []
    for i in range(1, n_tile):
        stat_copies.append(
            pltpu.make_async_remote_copy(
                stat, stats.at[i], stat_ssem.at[i], stat_rsem.at[i],
                device_id={"tile": (tile + i) % n_tile}, device_id_type=MESH,
            )
        )

    signal_tile(row_in, right)
    pl.semaphore_wait(row_in, 1)
    signal_tile(col_in.at[0], front)
    signal_tile(col_in.at[1], back)
    pl.semaphore_wait(col_in.at[0], 1)
    pl.semaphore_wait(col_in.at[1], 1)
    signal_tile(col_in.at[2], front)
    pl.semaphore_wait(col_in.at[2], 1)
    for copy in stat_copies:
        copy.start()

    for copy in stat_copies:
        copy.wait()
    total = stat[...]
    for i in range(1, n_tile):
        total = total + stats[i]
    bgs[...] = mean(total)
    delta[...] = bgs[...] - local[...]
    off = delta[0:4, :]
    parts = []
    for k in range(2):
        r, c = 8 * k, 16 + 8 * k
        part = raw[c : c + 4, :] + pltpu.roll(raw[r : r + 4, :] * off, 32, 1)
        part = part + pltpu.roll(raw[c + 4 : c + 8, :], 64, 1) + pltpu.roll(raw[r + 4 : r + 8, :] * off, 96, 1)
        parts.append(part)
    msg[...] = jnp.concatenate(parts, axis=0).astype(BF16)

    def msg_copy(p, c):
        target = 2 * ((z + distance(p) + n_z) % n_z) + c
        return pltpu.make_async_remote_copy(
            msg, msgs.at[p, core], msg_ssem.at[p, c], msg_rsem.at[p, core],
            device_id={"cuts": target}, device_id_type=MESH,
        )

    for p in range(EARLY):
        for c in range(2):
            msg_copy(p, c).start()

    level = fill_field(bgs)
    fill_halo(level)
    for q in range(1, n_z // 4):
        for s in range(n_s):
            filtered(q, s)
        for p in range(4 * q, 4 * q + 4):
            pack_one(p)
        for p in range(4 * q, 4 * q + 4):
            start_one(p)

    own = pltpu.make_async_copy(send.at[15, core], recv.at[15, core], osem)
    own.start()

    for load in small[2:]:
        load.wait()

    both = jnp.concatenate([amp[...].astype(F32).T, like[...].astype(F32).T], axis=0).astype(BF16)
    at = lax.broadcasted_iota(jnp.int32, (8, 512), 1)

    def tall(x):
        return jnp.concatenate([x] * 16, axis=0)

    def source_slice(pos, source_core, inner):
        dist = jnp.zeros_like(pos)
        for p in range(n_z):
            dist = jnp.where(pos == p, ORDER[p], dist)
        return 8 * ((z - dist + 2 * n_z) & (n_z - 1)) + 4 * source_core + inner

    inner = (at >> 2) & 3
    inner = inner + core * (1 - 2 * (inner & 1))
    slices = tall(source_slice(at >> 5, (at >> 4) & 1, inner))
    row_of = tall(at & 3)
    down_at = lax.broadcasted_iota(jnp.int32, (128, 512), 0)
    for r in range(4):
        pick = jnp.where(jnp.logical_and(slices == down_at, row_of == r), 1.0, 0.0).astype(BF16)
        wmat[256 * r : 256 * r + 256, :] = jnp.dot(both, pick, preferred_element_type=F32).astype(BF16)

    for i in range(2):
        absent = hrecv[i, 0].astype(F32) > 0.5 * ABSENT
        seen[n_row + 8 if i == 0 else 0 : n_row + 16 if i == 0 else 8, :] = (
            jnp.where(absent, 0.0, 1.0)
        )
    seen[8 : n_row + 8, :] = valid[...].astype(F32)
    seen[n_row + 16 : n_row + 24, :] = jnp.zeros((8, n_col), F32)
    window = seen[pl.ds(pl.multiple_of(8 * z, 8), 32), :]
    window = jnp.where(core == 0, window[0:24], pltpu.roll(window, 28, 0)[0:24])
    window = jnp.concatenate([window, jnp.zeros((24, 128), F32)], axis=1)
    for j in range(TAPS):
        turned = pltpu.roll(window, (REACH - j) % (n_col + 128), 1) if j != REACH else window
        shifted[24 * j : 24 * j + 24, :] = turned[:, 0:n_col]
    shifted[24 * TAPS : 512, :] = jnp.zeros((512 - 24 * TAPS, n_col), F32)

    for p in range(EARLY):
        for c in range(2):
            msg_copy(p, c).wait_send()
            pltpu.make_async_remote_copy(
                msg, msgs.at[p, c], msg_ssem.at[p, c], msg_rsem.at[p, c],
                device_id={"cuts": me}, device_id_type=MESH,
            ).wait_recv()

    column = jnp.zeros_like(at)
    for j in range(1, 22):
        column = column + jnp.where(at >= 24 * j, 1, 0)
    row = at - 24 * column
    column, row = tall(column), tall(row)
    terms = msgs[...].reshape(64, 128)

    def spread(lane_of):
        return jnp.dot(terms, jnp.where(down_at == lane_of, 1.0, 0.0).astype(BF16), preferred_element_type=F32)

    at = lax.broadcasted_iota(jnp.int32, (128, 64), 1)
    wanted = source_slice(at >> 4, (at >> 3) & 1, at & 3) == lax.broadcasted_iota(jnp.int32, (128, 64), 0)
    mixed = jnp.dot(both, jnp.where(wanted, 1.0, 0.0).astype(BF16), preferred_element_type=F32).astype(BF16)
    col_terms = [spread(column + 64 * k) for k in range(2)]
    for r in range(4):
        product = col_terms[0] * spread(32 + row - r) + col_terms[1] * spread(96 + row - r)
        gmat[256 * r : 256 * r + 256, :] = -jnp.dot(mixed, product.astype(BF16), preferred_element_type=F32)

    def correct(j, carry):
        lanes = pl.ds(pl.multiple_of(256 * j, 256), 256)
        acc[:, lanes] = jnp.dot(gmat[...].astype(BF16), shifted[:, lanes].astype(BF16), preferred_element_type=F32)
        return carry

    lax.fori_loop(0, n_col // 256, correct, 0)

    own.wait()
    for p in range(n_z):
        for c in range(2):

            def finish():
                block_copy(p, c).wait_send()
                pltpu.make_async_remote_copy(
                    send.at[p, c], recv.at[p, c], ssem.at[p, c], rsem.at[p, c],
                    device_id={"cuts": me}, device_id_type=MESH,
                ).wait_recv()

            if p == SELF:
                pl.when(c != core)(finish)
            else:
                finish()


def project_kernel(blocks, weights, acc, amp_out, like_out, amps, likes, sems):
    copies = []
    for j in range(4):
        part = blocks[:, :, :, 256 * j : 256 * j + 256].reshape(512, 256)
        both = jnp.dot(weights[...], part, preferred_element_type=F32) + acc[:, 256 * j : 256 * j + 256]
        for r in range(4):
            amp_float = both[256 * r : 256 * r + 128]
            like_float = amp_float * both[256 * r + 128 : 256 * r + 256]
            at = pl.ds(1024 * r + 256 * j, 256)
            amps[:, at] = amp_float.astype(BF16)
            likes[:, at] = like_float.astype(BF16)
            for i, (kept, out) in enumerate(((amps, amp_out), (likes, like_out))):
                copy = pltpu.make_async_copy(kept.at[:, at], out.at[:, at], sems.at[i, j, r])
                copy.start()
                copies.append(copy)
    for copy in copies:
        copy.wait()


def per_device(density, valid, row_taps, col_taps, amp_matrix, like_matrix):
    vmem = pl.BlockSpec(memory_space=pltpu.VMEM)
    anywhere = pl.BlockSpec(memory_space=pl.ANY)
    dma = pltpu.SemaphoreType.DMA
    blocks, weights, acc = pl.pallas_call(
        exchange_kernel,
        out_shape=(
            pltpu.VMEM((16, 2, 16, 1024), BF16),
            pltpu.VMEM((1024, 512), BF16),
            pltpu.VMEM((1024, 1024), F32),
        ),
        in_specs=[pl.BlockSpec(memory_space=pltpu.HBM)] * 6,
        out_specs=(vmem, vmem, vmem),
        scratch_shapes=[
            pltpu.VMEM((4, 128, 1024), BF16),
            pltpu.VMEM((128, 1024), jnp.int32),
            pltpu.VMEM((4, 4, 17), BF16),
            pltpu.VMEM((4, 4, 17), BF16),
            pltpu.VMEM((128, 128), BF16),
            pltpu.VMEM((128, 128), BF16),
            pltpu.VMEM((32, 256), F32),
            pltpu.VMEM((4, 4, 128, 256), BF16),
            pltpu.VMEM((4, 128, 1024), BF16),
            pltpu.VMEM((4, 256, 1024), BF16),
            pltpu.VMEM((4, 8, 32, 1024), BF16),
            pltpu.VMEM((4, 8, 32, 128), F32),
            pltpu.VMEM((16, 2, 16, 1024), BF16),
            pltpu.VMEM((8, 128), F32),
            pltpu.VMEM((16, 8, 128), F32),
            pltpu.VMEM((8, 128), F32),
            pltpu.VMEM((2, 4, 8, 1024), BF16),
            pltpu.VMEM((2, 4, 8, 1024), BF16),
            pltpu.VMEM((32, 128), F32),
            pltpu.VMEM((8, 128), F32),
            pltpu.VMEM((8, 128), F32),
            pltpu.VMEM((8, 128), BF16),
            pltpu.VMEM((EARLY, 2, 8, 128), BF16),
            pltpu.VMEM((152, 1024), F32),
            pltpu.VMEM((512, 1024), F32),
            pltpu.VMEM((1024, 512), F32),
            dma((16,)), dma((16,)), dma((2,)), dma((2,)),
            dma((16, 2)), dma((16, 2)), dma, dma, dma((4,)), dma((4,)),
            pltpu.SemaphoreType.REGULAR, pltpu.SemaphoreType.REGULAR((3,)),
            dma((EARLY, 2)), dma((EARLY, 2)),
        ],
        compiler_params=pltpu.CompilerParams(
            collective_id=0, has_side_effects=True, vmem_limit_bytes=44 * 1024 * 1024
        ),
        name="filter_exchange",
    )(*(
        pltpu.with_memory_space_constraint(x, pltpu.HBM)
        for x in (density, valid, row_taps, col_taps, amp_matrix, like_matrix)
    ))
    out = jax.ShapeDtypeStruct((128, 4096), BF16)
    return pl.pallas_call(
        project_kernel,
        out_shape=(out, out),
        in_specs=[vmem] * 3,
        out_specs=(anywhere, anywhere),
        scratch_shapes=[pltpu.VMEM((128, 4096), BF16), pltpu.VMEM((128, 4096), BF16), dma((2, 4, 4))],
        compiler_params=pltpu.CompilerParams(vmem_limit_bytes=44 * 1024 * 1024),
        name="project",
    )(
        pltpu.with_memory_space_constraint(blocks, pltpu.VMEM),
        pltpu.with_memory_space_constraint(weights, pltpu.VMEM),
        pltpu.with_memory_space_constraint(acc, pltpu.VMEM),
    )


def solution(mesh):
    return jax.shard_map(
        per_device,
        mesh=mesh,
        in_specs=(
            P("cuts", "tile", None),
            P("tile", None),
            P(None, "cuts", None),
            P(None, "cuts", None),
            P(),
            P(),
        ),
        out_specs=(P(None, ("tile", "cuts")), P(None, ("tile", "cuts"))),
        check_vma=False,
    )
```

time: 76 us -> 68.3 us (0.90)
  Pallas kernels: 75.2 us -> 67.5 us
    pallas_call x1, Pallas kernels: 72.7 us -> 65.1 us  [per_device(): pl.pallas_call(exchange_kernel, out_shape=(pltpu.VMEM((16, 2, 16, 1024),...]
where the time goes in v3:
time: 68.3 us; the launch traced here: 68.2 us
  Pallas kernels  67.5 us (99%)
    pallas_call x1, Pallas kernels, per_device(): pl.pallas_call(exchange_kernel, out_shape=(pltpu.VMEM((16, 2, 16, 1024),...  65.1 us
    pallas_call x1, Pallas kernels, per_device(): pl.pallas_call(project_kernel, out_shape=(out, out), in_specs=[vmem] * 3,...  2.43 us

profile of v3, /device:TPU:1, one launch (start us, length us, event | category | flops | bytes accessed | tf_op | source)
XLA Modules:
  0.0 68.2 jit_solution(13368947731172252657)
XLA Ops:
  0.6 65.1 %filter_exchange.1 = (bf16[16,2,16,1024]{3,2,1,0:T(8,128)(2,1)S(1)}, bf16[1024,512]{1,0:T(8,128)(2,1)S(1)}, f32[1024,1024]{1,0:T(8,128)S(1)}) custom-call(bf16[4,128,1024]{2,1,0:T(8,128)(2,1)} %dens_in.1, s32[128,1024]{1,0:T(8,128)} %valid_in.1, bf16[4,4,17]{2,1,0:T(4,128)(2,1)} %rtap_in.1, bf16[4,4,17]{2,1,0:T(4,128)(2,1)} %ctap_in.1, ...), custom_call_target="tpu_custom_call" | custom-call | tf_op jit(solution)/shard_map/filter_exchange/pallas_call | solution.py:423
  65.8 2.4 %project.1 = (bf16[128,4096]{1,0:T(8,128)(2,1)}, bf16[128,4096]{1,0:T(8,128)(2,1)}) custom-call(bf16[16,2,16,1024]{3,2,1,0:T(8,128)(2,1)S(1)} %get-tuple-element.5.blocks, bf16[1024,512]{1,0:T(8,128)(2,1)S(1)} %get-tuple-element.6.weights, f32[1024,1024]{1,0:T(8,128)S(1)} %get-tuple-element.7.acc), custom_call_target="tpu_custom_call" | custom-call | tf_op jit(solution)/shard_map/project/pallas_call | solution.py:473

commit v4 on v3

--- a/solution.py
+++ b/solution.py
@@ -373,18 +373,10 @@
         product = col_terms[0] * spread(32 + row - r) + col_terms[1] * spread(96 + row - r)
         gmat[256 * r : 256 * r + 256, :] = -jnp.dot(mixed, product.astype(BF16), preferred_element_type=F32)
 
-    def correct(j, carry):
-        lanes = pl.ds(pl.multiple_of(256 * j, 256), 256)
-        acc[:, lanes] = jnp.dot(gmat[...].astype(BF16), shifted[:, lanes].astype(BF16), preferred_element_type=F32)
-        return carry
-
-    lax.fori_loop(0, n_col // 256, correct, 0)
-
-    own.wait()
-    for p in range(n_z):
+    def finish(p):
         for c in range(2):
 
-            def finish():
+            def ended():
                 block_copy(p, c).wait_send()
                 pltpu.make_async_remote_copy(
                     send.at[p, c], recv.at[p, c], ssem.at[p, c], rsem.at[p, c],
@@ -392,16 +384,33 @@
                 ).wait_recv()
 
             if p == SELF:
-                pl.when(c != core)(finish)
+                pl.when(c != core)(ended)
             else:
-                finish()
+                ended()
+
+    half = n_z // 2
+    for p in range(half):
+        finish(p)
+
+    def correct(j, carry):
+        lanes = pl.ds(pl.multiple_of(256 * j, 256), 256)
+        early = jnp.dot(gmat[...].astype(BF16), shifted[:, lanes].astype(BF16), preferred_element_type=F32)
+        part = recv[0:half, :, :, lanes].reshape(256, 256)
+        acc[:, lanes] = early + jnp.dot(wmat[:, 0:256], part, preferred_element_type=F32)
+        return carry
+
+    lax.fori_loop(0, n_col // 256, correct, 0)
+
+    own.wait()
+    for p in range(half, n_z):
+        finish(p)
 
 
 def project_kernel(blocks, weights, acc, amp_out, like_out, amps, likes, sems):
     copies = []
     for j in range(4):
-        part = blocks[:, :, :, 256 * j : 256 * j + 256].reshape(512, 256)
-        both = jnp.dot(weights[...], part, preferred_element_type=F32) + acc[:, 256 * j : 256 * j + 256]
+        part = blocks[8:16, :, :, 256 * j : 256 * j + 256].reshape(256, 256)
+        both = jnp.dot(weights[:, 256:512], part, preferred_element_type=F32) + acc[:, 256 * j : 256 * j + 256]
         for r in range(4):
             amp_float = both[256 * r : 256 * r + 128]
             like_float = amp_float * both[256 * r + 128 : 256 * r + 256]

time: 68.3 us -> 67.8 us (level)
  no operation moved by 1% of the time
where the time goes in v4:
time: 67.8 us; the launch traced here: 67.7 us
  Pallas kernels  67 us (99%)
    pallas_call x1, Pallas kernels, per_device(): pl.pallas_call(exchange_kernel, out_shape=(pltpu.VMEM((16, 2, 16, 1024),...  65.1 us
    pallas_call x1, Pallas kernels, per_device(): pl.pallas_call(project_kernel, out_shape=(out, out), in_specs=[vmem] * 3,...  1.91 us

profile of v4, /device:TPU:1, one launch (start us, length us, event | category | flops | bytes accessed | tf_op | source)
XLA Modules:
  0.0 67.7 jit_solution(11799304645118985665)
XLA Ops:
  0.6 65.1 %filter_exchange.1 = (bf16[16,2,16,1024]{3,2,1,0:T(8,128)(2,1)S(1)}, bf16[1024,512]{1,0:T(8,128)(2,1)S(1)}, f32[1024,1024]{1,0:T(8,128)S(1)}) custom-call(bf16[4,128,1024]{2,1,0:T(8,128)(2,1)} %dens_in.1, s32[128,1024]{1,0:T(8,128)} %valid_in.1, bf16[4,4,17]{2,1,0:T(4,128)(2,1)} %rtap_in.1, bf16[4,4,17]{2,1,0:T(4,128)(2,1)} %ctap_in.1, ...), custom_call_target="tpu_custom_call" | custom-call | tf_op jit(solution)/shard_map/filter_exchange/pallas_call | solution.py:432
  65.8 1.9 %project.1 = (bf16[128,4096]{1,0:T(8,128)(2,1)}, bf16[128,4096]{1,0:T(8,128)(2,1)}) custom-call(bf16[16,2,16,1024]{3,2,1,0:T(8,128)(2,1)S(1)} %get-tuple-element.5.blocks, bf16[1024,512]{1,0:T(8,128)(2,1)S(1)} %get-tuple-element.6.weights, f32[1024,1024]{1,0:T(8,128)S(1)} %get-tuple-element.7.acc), custom_call_target="tpu_custom_call" | custom-call | tf_op jit(solution)/shard_map/project/pallas_call | solution.py:482

commit v5 on v4

--- a/solution.py
+++ b/solution.py
@@ -14,7 +14,7 @@
 F32 = jnp.float32
 BF16 = jnp.bfloat16
 
-ORDER = (7, -7, 6, -6, 8, 5, -5, 4, -4, 3, -3, 2, -2, 1, -1, 0)
+ORDER = (6, -6, 7, -7, 8, 5, -5, 4, -4, 3, -3, 2, -2, 1, -1, 0)
 EARLY = 4
 SELF = 15
 

time: 67.8 us -> 67.7 us (level)
  no operation moved by 1% of the time
where the time goes in v5:
time: 67.7 us; the launch traced here: 67.5 us
  Pallas kernels  66.9 us (99%)
    pallas_call x1, Pallas kernels, per_device(): pl.pallas_call(exchange_kernel, out_shape=(pltpu.VMEM((16, 2, 16, 1024),...  65 us
    pallas_call x1, Pallas kernels, per_device(): pl.pallas_call(project_kernel, out_shape=(out, out), in_specs=[vmem] * 3,...  1.9 us

profile of v5, /device:TPU:1, one launch (start us, length us, event | category | flops | bytes accessed | tf_op | source)
XLA Modules:
  0.0 67.5 jit_solution(6054141985420823218)
XLA Ops:
  0.6 65.0 %filter_exchange.1 = (bf16[16,2,16,1024]{3,2,1,0:T(8,128)(2,1)S(1)}, bf16[1024,512]{1,0:T(8,128)(2,1)S(1)}, f32[1024,1024]{1,0:T(8,128)S(1)}) custom-call(bf16[4,128,1024]{2,1,0:T(8,128)(2,1)} %dens_in.1, s32[128,1024]{1,0:T(8,128)} %valid_in.1, bf16[4,4,17]{2,1,0:T(4,128)(2,1)} %rtap_in.1, bf16[4,4,17]{2,1,0:T(4,128)(2,1)} %ctap_in.1, ...), custom_call_target="tpu_custom_call" | custom-call | tf_op jit(solution)/shard_map/filter_exchange/pallas_call | solution.py:432
  65.6 1.9 %project.1 = (bf16[128,4096]{1,0:T(8,128)(2,1)}, bf16[128,4096]{1,0:T(8,128)(2,1)}) custom-call(bf16[16,2,16,1024]{3,2,1,0:T(8,128)(2,1)S(1)} %get-tuple-element.5.blocks, bf16[1024,512]{1,0:T(8,128)(2,1)S(1)} %get-tuple-element.6.weights, f32[1024,1024]{1,0:T(8,128)S(1)} %get-tuple-element.7.acc), custom_call_target="tpu_custom_call" | custom-call | tf_op jit(solution)/shard_map/project/pallas_call | solution.py:482
